TPU v7x, 32 devices: a whole 2x2x4 slice. The times are simulated.
32 devices in a mesh: lat: 16 (over z, y, x), field: 2 (over core).
Axes of the slice: x: 2, y: 2, z: 4, core: 2. Of those that a mesh axis runs over, the one named last changes fastest.
Arguments:
- fields_grid: bfloat16 [2, 64, 2, 48, 192], P('field', None, None, 'lat'), may hold values from -6 to 6
- basis: bfloat16 [128, 48, 96], P('lat'), may hold values from -0.875 to 0.875
- order_table: int32 [16, 8], replicated, may hold values from -1 to 95, as said below
- panel_modes: int32 [2, 64], replicated, may hold values from 0 to 95, as said below
Outputs:
- panel: bfloat16 [2, 128, 192, 128], P('field', 'lat')
Inputs may be any that keep to these rules, and one draw needn't show every extreme that they name: `order_table`: each order 0 to 95 stands in exactly one slot; every other slot holds -1; some group has all 8 slots filled. `panel_modes`: row 1 is never smaller than row 0 in the same column; degree 95 appears.
All inputs are finite; a program needn't handle non-finite values.
Results may differ from a plain program's by a relative error of at most 0.0082.
Values may be sent and summed in bfloat16 or wider, within the bound.
A program may use at most 64 MiB of HBM per device.

v0:
```python
import functools
import math

import jax
import jax.numpy as jnp
import numpy as np
from jax import lax
from jax.experimental import pallas as pl
from jax.experimental.pallas import tpu as pltpu
from jax.sharding import PartitionSpec as P

BF = jnp.bfloat16
F32 = jnp.float32
NT = (((1,), (1,)), ((), ()))


def iota(shape, dim):
    return lax.broadcasted_iota(jnp.int32, shape, dim)


def mm(a, b):
    return jnp.dot(a, b, preferred_element_type=F32)


def mm_nt(a, b):
    return lax.dot_general(a, b, NT, preferred_element_type=F32)


def kernel(
    lat_count, snap, pairs, lon, slots, degs, per_dev, tail,
    x_hbm, basis_hbm, table_hbm, orders_hbm, modes_hbm,
    coef_hbm, twice_ref,
    x_ref, basis_ref, table_ref, orders_ref, modes_ref, load_sem,
    send, recv, tail_send, tail_recv, mode_send, mode_recv, perm, rows,
    send_sem, recv_sem, tail_send_sem, tail_recv_sem, mode_send_sem, mode_recv_sem,
):
    me = lax.axis_index("lat")
    field = lax.axis_index("field")
    other = 1 - field
    pair_total = lat_count * pairs
    width = 2 * snap
    block = 2 * slots
    head = pairs * block
    all_rows = lat_count * block
    tail_rows = lat_count * tail
    used = pairs * per_dev

    loads = [
        pltpu.make_async_copy(src, dst, load_sem.at[at])
        for at, (src, dst) in enumerate([
            (orders_hbm, orders_ref), (modes_hbm, modes_ref), (table_hbm, table_ref),
            (x_hbm, x_ref), (basis_hbm, basis_ref),
        ])
    ]
    for load in loads:
        load.start()

    barrier = pltpu.get_barrier_semaphore()

    def greet_own(k, c):
        pl.semaphore_signal(barrier, inc=1, device_id=(lax.rem(me + k, lat_count), field),
                            device_id_type=pl.DeviceIdType.MESH)
        return c

    def greet_other(k, c):
        pl.semaphore_signal(barrier, inc=1, device_id=(lax.rem(me + k, lat_count), other),
                            device_id_type=pl.DeviceIdType.MESH)
        return c

    lax.fori_loop(1, lat_count, greet_own, 0)
    lax.fori_loop(0, lat_count, greet_other, 0)

    nord = table_ref.shape[0] // 2
    loads[0].wait()
    loads[1].wait()
    by_slot = orders_ref[...]
    tiled = jnp.concatenate([by_slot] * (2 * lat_count), axis=0)
    here = iota((all_rows, lat_count), 1) == iota((all_rows, lat_count), 0) // block
    order_col = jnp.sum(jnp.where(here, tiled, 0), axis=1, keepdims=True)
    mode_total = lat_count * per_dev
    mode_row = iota((tail_rows, mode_total), 0)
    mode_here = iota((tail_rows, mode_total), 1) == mode_row // tail * per_dev + mode_row % per_dev
    mode_col = jnp.sum(jnp.where(mode_here, modes_ref[0:1, :], 0), axis=1, keepdims=True)
    deg_col = jnp.sum(jnp.where(mode_here, modes_ref[1:2, :], 0), axis=1, keepdims=True)
    my_orders = jnp.sum(
        jnp.where(iota((slots, lat_count), 1) == me, by_slot, 0), axis=1, keepdims=True
    )
    group_of = (iota((lat_count, all_rows), 1) // block == iota((lat_count, all_rows), 0))
    by_lane = mm(by_slot.astype(F32).astype(BF), group_of.astype(F32).astype(BF))
    slot_of = iota((slots, all_rows), 1) % slots == iota((slots, all_rows), 0)
    row_order = jnp.sum(jnp.where(slot_of, by_lane, 0.0), axis=0, keepdims=True).astype(jnp.int32)
    parity_row = iota((all_rows, 1), 0) // slots % 2
    want = jnp.where(order_col >= 0, order_col + nord * parity_row, -1)
    onehot = (iota((all_rows, 2 * nord), 1) == want).astype(F32).astype(BF)
    loads[2].wait()
    dft = mm(onehot, table_ref[...]).astype(BF)
    rho = iota((tail_rows, 1), 0) % tail
    row_parity = iota((1, all_rows), 1) // slots % 2
    mode_parity = (deg_col - mode_col) % 2
    match = (mode_col == row_order) & (mode_parity == row_parity)
    tail_acc = jnp.zeros((tail_rows, width), F32)
    zero_x = jnp.zeros((snap, 2 * lon), BF)
    loads[3].wait()
    for j in range(pairs):
        xj = jnp.concatenate([x_ref[:, j, 0, :], x_ref[:, j, 1, :]], axis=1)
        both = jnp.concatenate(
            [jnp.concatenate([xj, zero_x], axis=1), jnp.concatenate([zero_x, xj], axis=1)], axis=0
        )
        part = (mm_nt(dft, both) * (1.0 / math.sqrt(lon))).astype(BF)
        send[:, j * block:(j + 1) * block, :] = part.reshape(lat_count, block, width)
        mine = match & (rho // per_dev == j)
        tail_acc = tail_acc + mm(mine.astype(F32).astype(BF), part)
    at_degree = (iota((tail_rows, degs), 1) == deg_col) & (rho >= used) & (rho < used + per_dev)
    loads[4].wait()
    basis_acc = jnp.zeros((tail_rows, pair_total), F32)
    for s in range(slots):
        pick = at_degree & (mode_col == my_orders[s:s + 1, :])
        basis_acc = basis_acc + mm_nt(pick.astype(F32).astype(BF), basis_ref[s])
    wide = jnp.concatenate(
        [basis_acc, jnp.zeros((tail_rows, width - pair_total), F32)], axis=1
    )
    tail_all = (tail_acc + wide).astype(BF)
    tail_send[...] = tail_all.reshape(lat_count, tail, width)

    pl.semaphore_wait(barrier, 2 * lat_count - 1)

    def whole(src, dst, count, one_send_sem, one_recv_sem):
        return pltpu.make_async_remote_copy(
            src_ref=src.at[pl.ds(0, count)], dst_ref=dst.at[pl.ds(0, count)],
            send_sem=one_send_sem, recv_sem=one_recv_sem,
            device_id=(me, other), device_id_type=pl.DeviceIdType.MESH,
        )

    def block_copy(dst, src):
        return pltpu.make_async_remote_copy(
            src_ref=send.at[dst], dst_ref=recv.at[src],
            send_sem=send_sem, recv_sem=recv_sem,
            device_id=(dst, field), device_id_type=pl.DeviceIdType.MESH,
        )

    def tail_copy(dst, src):
        return pltpu.make_async_remote_copy(
            src_ref=tail_send.at[dst], dst_ref=tail_recv.at[src],
            send_sem=tail_send_sem, recv_sem=tail_recv_sem,
            device_id=(dst, field), device_id_type=pl.DeviceIdType.MESH,
        )

    def start_tail(k, c):
        tail_copy(lax.rem(me + k, lat_count), me).start()
        return c

    lax.fori_loop(1, lat_count, start_tail, 0)

    def start_block(k, c):
        block_copy(lax.rem(me + k, lat_count), me).start()
        return c

    lax.fori_loop(1, lat_count, start_block, 0)
    recv[me] = send[me]
    tail_recv[me] = tail_send[me]

    src_of = iota((width, tail_rows), 1) // tail
    rho_of = iota((width, tail_rows), 1) % tail
    spread = (
        (iota((width, tail_rows), 0) == src_of * pairs + rho_of // per_dev) & (rho_of < used)
    ).astype(F32).astype(BF)
    own_row = iota((per_dev, tail_rows), 0) == iota((per_dev, tail_rows), 1) % tail % per_dev

    k_rows = slots * 2 * pair_total
    for s in range(slots):
        shape = (2 * pair_total, k_rows // 1)
        r = iota((2 * pair_total, 1), 0)
        p = r // pair_total
        j = r % pair_total
        target = j * block + p * slots + s
        perm[s * 2 * pair_total:(s + 1) * 2 * pair_total, :] = (
            iota((2 * pair_total, lat_count * head), 1) == target
        ).astype(F32).astype(BF)
    dup = (iota((2 * degs, degs), 0) // 2 == iota((2 * degs, degs), 1)).astype(F32).astype(BF)
    for s in range(slots):
        order = my_orders[s:s + 1, :]
        deg = iota((2 * degs, pair_total), 0) // 2
        base = mm_nt(dup, basis_ref[s])
        keep = (deg >= order) & (order >= 0)
        odd = (deg - order) % 2
        even_part = jnp.where(keep & (odd == 0), base, 0.0)
        odd_part = jnp.where(keep & (odd == 1), base, 0.0)
        rows[s] = jnp.concatenate([even_part, odd_part], axis=1).astype(BF)
    all_tails = whole(tail_send, tail_recv, lat_count - 1, tail_send_sem, tail_recv_sem)
    all_tails.wait_recv()

    tails = tail_recv[...]
    summed = jnp.sum(tails.astype(F32), axis=0)[used:used + per_dev].astype(BF)
    weights = jnp.where(own_row, mm(summed, spread), 0.0).astype(BF)
    mode_send[...] = mm(weights, tails.reshape(tail_rows, width)).astype(BF)

    def mode_copy(dst, src):
        return pltpu.make_async_remote_copy(
            src_ref=mode_send, dst_ref=mode_recv.at[src],
            send_sem=mode_send_sem, recv_sem=mode_recv_sem,
            device_id=(dst, other), device_id_type=pl.DeviceIdType.MESH,
        )

    def start_mode(k, c):
        mode_copy(lax.rem(me + k, lat_count), me).start()
        return c

    lax.fori_loop(0, lat_count, start_mode, 0)

    all_blocks = whole(send, recv, lat_count - 1, send_sem, recv_sem)
    all_blocks.wait_recv()

    heads = recv[...].reshape(lat_count * head, width)
    sorted_rows = mm(perm[...], heads).astype(BF)
    same_r = iota((2 * degs, width), 1) // snap == iota((2 * degs, width), 0) % 2
    for s in range(slots):
        value = mm(rows[s], sorted_rows[s * 2 * pair_total:(s + 1) * 2 * pair_total])
        coef_hbm[s] = jnp.where(same_r, value, 0.0).astype(BF)

    modes = lat_count * per_dev
    expand = (iota((2 * modes, modes), 1) == iota((2 * modes, modes), 0) // 2).astype(F32).astype(BF)

    all_modes = whole(mode_recv, mode_recv, lat_count, mode_send_sem, mode_recv_sem)
    all_modes.wait_recv()
    values = mode_recv[...].reshape(modes, width)
    columns = mm(expand, values)
    u_match = iota((2 * modes, width), 1) // snap == iota((2 * modes, width), 0) % 2
    masked = jnp.where(u_match, columns, 0.0)
    mean = jnp.sum(masked, axis=1, keepdims=True) * (1.0 / snap)
    centered = jnp.where(u_match, masked - mean, 0.0)
    twice_ref[...] = (centered + pltpu.roll(centered, snap, 1)).astype(BF)

    all_blocks.wait_send()
    all_tails.wait_send()
    all_modes.wait_send()


def dft_constant(nord, lon):
    angles = (np.outer(np.arange(nord), np.arange(lon)) % lon) * (2.0 * math.pi / lon)
    cosine, sine = np.cos(angles), -np.sin(angles)
    even = np.concatenate([cosine, cosine, sine, sine], axis=1)
    odd = np.concatenate([cosine, -cosine, sine, -sine], axis=1)
    return np.concatenate([even, odd], axis=0).astype(np.float32).astype(BF)


def fused(lat_count, tail, fields_grid, basis, order_table, panel_modes):
    _, snap, _, pairs, lon = fields_grid.shape
    slots, pair_total, degs = basis.shape
    modes = panel_modes.shape[1]
    per_dev = modes // lat_count
    width = 2 * snap
    block = 2 * slots
    head = pairs * block
    x = fields_grid[0].transpose(0, 2, 1, 3)
    table = jnp.asarray(dft_constant(degs, lon))
    vmem = pl.BlockSpec(memory_space=pltpu.VMEM)
    body = functools.partial(kernel, lat_count, snap, pairs, lon, slots, degs, per_dev, tail)
    coef, twice = pl.pallas_call(
        body,
        out_shape=(
            jax.ShapeDtypeStruct((slots, 2 * degs, width), BF),
            jax.ShapeDtypeStruct((2 * modes, width), BF),
        ),
        in_specs=[pl.BlockSpec(memory_space=pl.ANY)] * 5,
        out_specs=(vmem, vmem),
        scratch_shapes=[
            pltpu.VMEM(x.shape, BF),
            pltpu.VMEM(basis.shape, BF),
            pltpu.VMEM(table.shape, BF),
            pltpu.VMEM((slots, lat_count), jnp.int32),
            pltpu.VMEM(panel_modes.shape, jnp.int32),
            pltpu.SemaphoreType.DMA((5,)),
            pltpu.VMEM((lat_count, head, width), BF),
            pltpu.VMEM((lat_count, head, width), BF),
            pltpu.VMEM((lat_count, tail, width), BF),
            pltpu.VMEM((lat_count, tail, width), BF),
            pltpu.VMEM((per_dev, width), BF),
            pltpu.VMEM((lat_count, per_dev, width), BF),
            pltpu.VMEM((slots * 2 * pair_total, lat_count * head), BF),
            pltpu.VMEM((slots, 2 * degs, 2 * pair_total), BF),
            pltpu.SemaphoreType.DMA,
            pltpu.SemaphoreType.DMA,
            pltpu.SemaphoreType.DMA,
            pltpu.SemaphoreType.DMA,
            pltpu.SemaphoreType.DMA,
            pltpu.SemaphoreType.DMA,
        ],
        compiler_params=pltpu.CompilerParams(
            collective_id=0, has_side_effects=True, vmem_limit_bytes=52 * 1024 * 1024
        ),
    )(*[pltpu.with_memory_space_constraint(v, pltpu.HBM) for v in (x, basis, table, order_table.T, panel_modes)])
    panel = lax.dot_general(
        coef.reshape(slots * 2 * degs, width), twice, NT, preferred_element_type=F32
    ) * (1.0 / (snap - 1))
    return panel.astype(BF).reshape(1, slots, 2 * degs, 2 * modes)


def dft_table(orders, lon_count):
    valid_slot = orders >= 0
    safe_orders = jnp.maximum(orders, 0)
    products = lax.broadcasted_iota(jnp.int32, (lon_count, 1), 0) * safe_orders[None, :] % lon_count
    angles = products.astype(jnp.float32) * (2.0 * math.pi / lon_count)
    cosine = jnp.where(valid_slot[None, :], jnp.cos(angles), 0.0).astype(jnp.bfloat16)
    sine_table = jnp.where(valid_slot[None, :], -jnp.sin(angles), 0.0).astype(jnp.bfloat16)
    return jnp.stack([cosine, sine_table], axis=1)


def local(fields_grid, basis, order_table, panel_modes):
    grid_one = fields_grid[0]
    snap_count = grid_one.shape[0]
    pair_count = grid_one.shape[2]
    lon_count = grid_one.shape[3]
    slot_count = order_table.shape[1]
    deg_count = basis.shape[2]
    pair_total = basis.shape[1]
    mode_count = panel_modes.shape[1]
    orders = order_table.reshape(-1)
    slot_all = orders.shape[0]
    dft = dft_table(orders, lon_count)
    fourier = jnp.einsum("thjn,nrk->hkjrt", grid_one, dft, preferred_element_type=jnp.float32) * (
        1.0 / math.sqrt(lon_count)
    )
    fourier = fourier.reshape(2, slot_all, pair_count, 2 * snap_count)
    parity_parts = jnp.stack([fourier[0] + fourier[1], fourier[0] - fourier[1]]).astype(
        jnp.bfloat16
    )
    group_index = lax.axis_index("lat")
    my_orders = lax.dynamic_slice_in_dim(order_table, group_index, 1, 0)[0]
    my_odd = my_orders % 2 == 1
    basis_split = basis.reshape(slot_count, pair_total, deg_count // 2, 2)
    even_rows = basis_split[:, :, :, 0]
    odd_rows = basis_split[:, :, :, 1]
    degree = lax.broadcasted_iota(jnp.int32, (1, deg_count), 1)
    keep_mask = (degree >= my_orders[:, None]) & (my_orders >= 0)[:, None]
    received = lax.all_to_all(parity_parts, "lat", split_axis=1, concat_axis=2, tiled=True)
    first_parity = jnp.where(my_odd[:, None, None], received[1], received[0])
    second = jnp.where(my_odd[:, None, None], received[0], received[1])
    low_degrees = jnp.einsum(
        "sjh,sjc->shc", even_rows, first_parity, preferred_element_type=jnp.float32
    )
    high_degrees = jnp.einsum("sjh,sjc->shc", odd_rows, second, preferred_element_type=jnp.float32)
    joined = jnp.stack([low_degrees, high_degrees], axis=2).reshape(slot_count, deg_count, -1)
    coefficients = jnp.where(keep_mask[:, :, None], joined, 0.0).astype(jnp.bfloat16)
    mode_order = panel_modes[0]
    mode_degree = panel_modes[1]
    onehot = (my_orders[None, :] == mode_order[:, None]).astype(jnp.bfloat16)
    picked = jnp.take(coefficients, mode_degree, axis=1)
    local_values = jnp.einsum("ms,smc->mc", onehot, picked, preferred_element_type=jnp.float32)
    field_index = lax.axis_index("field")
    both_fields = jnp.stack(
        [
            jnp.where(field_index == 0, local_values, 0.0),
            jnp.where(field_index == 1, local_values, 0.0),
        ]
    )
    summed = lax.psum(both_fields, ("lat", "field"))
    other_field = jnp.where(field_index == 0, summed[1], summed[0]).astype(jnp.bfloat16)
    columns = other_field.astype(jnp.float32).reshape(mode_count * 2, snap_count)
    centered = (columns - jnp.mean(columns, axis=1, keepdims=True)).astype(jnp.bfloat16)
    coef_rows = coefficients.reshape(slot_count * deg_count * 2, snap_count)
    panel_values = lax.dot_general(
        coef_rows, centered, (((1,), (1,)), ((), ())), preferred_element_type=jnp.float32
    )
    panel_values = panel_values * (1.0 / (snap_count - 1))
    return panel_values.astype(jnp.bfloat16).reshape(1, slot_count, 2 * deg_count, 2 * mode_count)


def device_program(lat_count, fields_grid, basis, order_table, panel_modes):
    pairs, snap = fields_grid.shape[3], fields_grid.shape[1]
    slots, pair_total, _ = basis.shape
    modes = panel_modes.shape[1]
    per_dev = modes // lat_count
    tail = (pairs + 1) * per_dev if per_dev else 0
    rows = slots * 2 * pair_total
    fits = (
        modes % lat_count == 0
        and tail == 2 * slots
        and tail % 16 == 0
        and 2 * snap == 128
        and slots == 8
        and basis.shape[2] <= 256
        and pair_total <= 2 * snap
        and rows * rows * 2 <= 8 * 1024 * 1024
    )
    if fits:
        return fused(lat_count, tail, fields_grid, basis, order_table, panel_modes)
    return local(fields_grid, basis, order_table, panel_modes)


def solution(mesh):
    placed = (P("field", None, None, "lat", None), P("lat", None, None), P(), P())
    return jax.shard_map(
        functools.partial(device_program, mesh.shape["lat"]),
        mesh=mesh, in_specs=placed, out_specs=P("field", "lat", None, None), check_vma=False,
    )
```

profile of v0, /device:TPU:1, one launch (start us, length us, event | category | flops | bytes accessed | tf_op | source)
XLA Modules:
  0.0 17.7 jit_solution(6981113068866899363)
XLA Ops:
  0.0 16.7 %shard_map.55 = (bf16[8,192,128]{2,1,0:T(8,128)(2,1)S(1)}, bf16[128,128]{1,0:T(8,128)(2,1)S(1)}) custom-call(bf16[64,3,2,192]{3,2,1,0:T(2,128)(2,1)} %bitcast.9, bf16[8,48,96]{2,1,0:T(8,128)(2,1)} %basis_hbm.1, bf16[192,768]{1,0:T(8,128)(2,1)} %constant.4.clone.table_hbm, s32[8,16]{1,0:T(8,128)} %bitcast.10, s32[2,64]{1,0:T(2,128)} %modes_hbm.1), custom_call_target="tpu_custom_call" | custom-call | tf_op jit(solution)/shard_map/pallas_call | solution.py:258
  16.7 1.0 %fusion = bf16[1536,128]{1,0:T(8,128)(2,1)} fusion(bf16[1536,128]{1,0:T(8,128)(2,1)S(1)} %bitcast.8, bf16[128,128]{1,0:T(8,128)(2,1)S(1)} %get-tuple-element.8), kind=kOutput, calls=%fused_computation.1 | convolution fusion | flops 50724864 | bytes 819200 | tf_op jit(solution)/shard_map/dot_general | solution.py:292
where the time goes:
time: 17.9 us; the launch traced here: 17.7 us
  Pallas kernels  16.7 us (93%)
  matrix products  1.01 us (6%)
    pallas_call x1, Pallas kernels, fused(): pl.pallas_call(body, out_shape=(jax.ShapeDtypeStruct((slots, 2 * degs, wi...  16.7 us
    dot_general x1, matrix products, fused(): lax.dot_general(coef.reshape(slots * 2 * degs, width), twice, NT, preferr...  1.01 us

commit v1 on v0

v1 whole, which is shorter than its diff:
```python
import functools
import math

import jax
import jax.numpy as jnp
import numpy as np
from jax import lax
from jax.experimental import pallas as pl
from jax.experimental.pallas import tpu as pltpu
from jax.sharding import PartitionSpec as P

BF = jnp.bfloat16
F32 = jnp.float32
NT = (((1,), (1,)), ((), ()))


def iota(shape, dim):
    return lax.broadcasted_iota(jnp.int32, shape, dim)


def mm(a, b):
    return jnp.dot(a, b, preferred_element_type=F32)


def mm_nt(a, b):
    return lax.dot_general(a, b, NT, preferred_element_type=F32)


def kernel(
    lat_count, snap, pairs, lon, slots, degs, first, owners, per,
    x_hbm, basis_hbm, table_hbm, orders_hbm, modes_hbm,
    coef_ref, twice_ref,
    x_ref, basis_ref, table_ref, orders_ref, modes_ref, load_sem,
    send, recv, tail_send, tail_recv, col_send, col_recv, mode_send, mode_recv, wide, rows,
    send_sem, recv_sem, tail_send_sem, tail_recv_sem, col_send_sem, col_recv_sem,
    mode_send_sem, mode_recv_sem, late,
):
    me = lax.axis_index("lat")
    field = lax.axis_index("field")
    other = 1 - field
    pair_total = lat_count * pairs
    width = 2 * snap
    block = 2 * slots
    slot_all = lat_count * slots
    modes = owners * per
    early = first + owners
    is_early = me < early
    in_owners = (me >= first) & (me < early)
    is_owner = in_owners & (field == 1)

    loads = [
        pltpu.make_async_copy(src, dst, load_sem.at[at])
        for at, (src, dst) in enumerate([
            (modes_hbm, modes_ref), (orders_hbm, orders_ref), (table_hbm, table_ref),
            (basis_hbm, basis_ref), (x_hbm, x_ref),
        ])
    ]
    for load in loads:
        load.start()

    barrier = pltpu.get_barrier_semaphore()

    def signal(sem, lat, core):
        pl.semaphore_signal(sem, inc=1, device_id=(lat, core), device_id_type=pl.DeviceIdType.MESH)

    def owns(lat):
        return (lat >= first) & (lat < early)

    def greet(lat, c):
        @pl.when((lat != me) & (is_early | (lat >= early)))
        def _():
            signal(barrier, lat, field)

        @pl.when(is_early & (is_owner | ((field == 0) & owns(lat))))
        def _():
            signal(barrier, lat, other)
        return c

    lax.fori_loop(0, lat_count, greet, 0)

    nord = table_ref.shape[0] // 2
    loads[0].wait()
    loads[1].wait()
    diagonal = iota((modes, modes), 0) == iota((modes, modes), 1)
    mode_col = jnp.sum(jnp.where(diagonal, modes_ref[0:1, :], 0), axis=1, keepdims=True)
    deg_col = jnp.sum(jnp.where(diagonal, modes_ref[1:2, :], 0), axis=1, keepdims=True)
    mode_odd = ((deg_col - mode_col) & 1) == 1
    by_slot = orders_ref[...]
    my_orders = jnp.sum(
        jnp.where(iota((slots, lat_count), 1) == me, by_slot, 0), axis=1, keepdims=True
    )

    def waves(cosine_row, sine_row):
        want = jnp.concatenate([cosine_row, sine_row], axis=0)
        onehot = (iota((want.shape[0], 2 * nord), 1) == want).astype(F32).astype(BF)
        return mm(onehot, table_ref[...]).astype(BF)

    loads[2].wait()
    mode_dft = waves(mode_col, mode_col + nord)
    loads[3].wait()
    cols = jnp.zeros((modes, pair_total), F32)
    at_degree = iota((modes, degs), 1) == deg_col
    for s in range(slots):
        pick = at_degree & (mode_col == my_orders[s:s + 1, :])
        cols = cols + mm_nt(pick.astype(F32).astype(BF), basis_ref[s])
    cols = jnp.concatenate([cols, jnp.zeros((modes, width - pair_total), F32)], axis=1)
    col_send[...] = cols.reshape(owners, per, width).astype(BF)
    even_lane = iota((1, width), 1) % 2 == 0

    def hemispheres(table, j):
        wave = mm_nt(table, x_ref[:, j].reshape(width, lon)) * (1.0 / math.sqrt(lon))
        half = wave.shape[0] // 2
        real, imag = wave[:half], wave[half:]
        north = jnp.where(even_lane, real, pltpu.roll(imag, 1, 1))
        south = jnp.where(even_lane, pltpu.roll(real, width - 1, 1), imag)
        return north, south

    loads[4].wait()
    for j in range(pairs):
        north, south = hemispheres(mode_dft, j)
        part = jnp.where(mode_odd, north - south, north + south)
        tail_send[:, j * per:(j + 1) * per, :] = part.reshape(owners, per, width).astype(BF)

    across = jnp.where(field == 0, owners, jnp.where(is_owner, early, 0))
    across_late = jnp.where(field == 0, owners, 0)
    pl.semaphore_wait(
        barrier, jnp.where(is_early, early - 1 + across, lat_count - 1 + across_late)
    )

    @pl.when(jnp.logical_not(is_early))
    def _():
        def arrive(lat, c):
            signal(late, lat, field)

            @pl.when((field == 0) & owns(lat))
            def _():
                signal(late, lat, other)
            return c

        lax.fori_loop(0, early, arrive, 0)

    def remote(src, dst, sems, lat, core):
        return pltpu.make_async_remote_copy(
            src_ref=src, dst_ref=dst, send_sem=sems[0], recv_sem=sems[1],
            device_id=(lat, core), device_id_type=pl.DeviceIdType.MESH,
        )

    block_sems = (send_sem, recv_sem)
    col_sems = (col_send_sem, col_recv_sem)

    def mode_sems(core):
        return (mode_send_sem.at[core], mode_recv_sem)

    def tail_sems(core):
        return (tail_send_sem, tail_recv_sem.at[core])

    def whole(ref, count, sems):
        part = ref.at[pl.ds(0, count)]
        return remote(part, part, sems, me, other)

    def start_tail(at, c):
        @pl.when((field == 1) & (at + first != me))
        def _():
            remote(col_send.at[at], col_recv.at[me], col_sems, at + first, 1).start()

        @pl.when((field == 0) | (at + first != me))
        def _():
            remote(tail_send.at[at], tail_recv.at[field, me], tail_sems(field), at + first, 1).start()
        return c

    lax.fori_loop(0, owners, start_tail, 0)

    tiled = jnp.concatenate([by_slot] * lat_count, axis=0)
    here = iota((slot_all, lat_count), 1) == iota((slot_all, lat_count), 0) // slots
    order_col = jnp.sum(jnp.where(here, tiled, 0), axis=1, keepdims=True)
    slot_dft = waves(order_col, jnp.where(order_col >= 0, order_col + nord, -1))
    for j in range(pairs):
        north, south = hemispheres(slot_dft, j)
        shape = (lat_count, slots, width)
        both = jnp.concatenate([(north + south).reshape(shape), (north - south).reshape(shape)], axis=1)
        send[:, j * block:(j + 1) * block, :] = both.astype(BF)

    def start_block(lat, c):
        @pl.when(lat != me)
        def _():
            remote(send.at[lat], recv.at[me], block_sems, lat, field).start()
        return c

    lax.fori_loop(0, first, start_block, 0)

    dup = (iota((2 * degs, degs), 0) // 2 == iota((2 * degs, degs), 1)).astype(F32).astype(BF)
    twin = (iota((pair_total, 2 * pair_total), 1) // 2 == iota((pair_total, 2 * pair_total), 0))
    twin = twin.astype(F32).astype(BF)
    deg = iota((2 * degs, 2 * pair_total), 0) // 2
    parity = iota((2 * degs, 2 * pair_total), 1) & 1
    for s in range(slots):
        order = my_orders[s:s + 1, :]
        base = mm(mm_nt(dup, basis_ref[s]).astype(BF), twin)
        keep = (deg >= order) & (order >= 0) & (((deg - order) & 1) == parity)
        rows[s] = jnp.where(keep, base, 0.0).astype(BF)

    lax.fori_loop(first, early, start_block, 0)

    @pl.when(is_early)
    def _():
        pl.semaphore_wait(late, (lat_count - early) * jnp.where(is_owner, 2, 1))

    lax.fori_loop(early, lat_count, start_block, 0)
    recv[me] = send[me]

    @pl.when(is_owner)
    def _():
        tail_recv[1, me] = tail_send[me - first]
        col_recv[me] = col_send[me - first]
        total = lat_count * pairs * per
        place = iota((width, total), 1)
        spread = iota((width, total), 0) == place // (pairs * per) * pairs + place // per % pairs
        own = iota((per, total), 0) == iota((per, total), 1) % per
        whole(col_recv, lat_count - 1, col_sems).wait_recv()
        column = jnp.sum(col_recv[...].astype(F32), axis=0).astype(BF)
        weights = jnp.where(own, mm(column, spread.astype(F32).astype(BF)), 0.0).astype(BF)

        def value_of(core):
            return mm(weights, tail_recv[core].reshape(total, width)).astype(BF)

        def start_mode(core):
            def start(lat, c):
                @pl.when((core == 0) | (lat != me))
                def _():
                    remote(
                        mode_send.at[1 - core], mode_recv.at[me - first], mode_sems(core), lat, core
                    ).start()
                return c

            lax.fori_loop(0, lat_count, start, 0)

        whole(tail_recv.at[1], lat_count - 1, tail_sems(1)).wait_recv()
        mode_send[1] = value_of(1)
        start_mode(0)
        whole(tail_recv.at[0], lat_count, tail_sems(0)).wait_recv()
        mode_send[0] = value_of(0)
        start_mode(1)
        mode_recv[me - first] = mode_send[0]

    whole(recv, lat_count - 1, block_sems).wait_recv()
    wide[...] = recv[...].reshape(slot_all * 2 * pairs, width).astype(F32)
    same_r = iota((2 * degs, width), 1) % 2 == iota((2 * degs, width), 0) % 2
    for s in range(slots):
        picked = wide[pl.ds(s, 2 * pair_total, stride=slots), :].astype(BF)
        coef_ref[s] = jnp.where(same_r, mm(rows[s], picked), 0.0).astype(BF)

    expand = (iota((2 * modes, modes), 1) == iota((2 * modes, modes), 0) // 2).astype(F32).astype(BF)
    u_match = iota((2 * modes, width), 1) % 2 == iota((2 * modes, width), 0) % 2
    row_even = iota((2 * modes, 1), 0) % 2 == 0

    @pl.when(is_owner)
    def _():
        whole(mode_recv, owners - 1, mode_sems(0)).wait_recv()

    @pl.when(jnp.logical_not(is_owner))
    def _():
        whole(mode_recv, owners, mode_sems(0)).wait_recv()

    columns = mm(expand, mode_recv[...].reshape(modes, width))
    masked = jnp.where(u_match, columns, 0.0)
    mean = jnp.sum(masked, axis=1, keepdims=True) * (1.0 / snap)
    centered = jnp.where(u_match, masked - mean, 0.0)
    moved = jnp.where(row_even, pltpu.roll(centered, 1, 1), pltpu.roll(centered, width - 1, 1))
    twice_ref[...] = (centered + moved).astype(BF)

    whole(send, lat_count - 1, block_sems).wait_send()

    @pl.when(is_owner)
    def _():
        whole(tail_send, owners - 1, tail_sems(field)).wait_send()
        whole(col_recv, lat_count, mode_sems(0)).wait_send()
        whole(col_recv, lat_count - 1, mode_sems(1)).wait_send()

    @pl.when(jnp.logical_not(is_owner))
    def _():
        whole(tail_send, owners, tail_sems(field)).wait_send()

    @pl.when((field == 1) & in_owners)
    def _():
        whole(col_send, owners - 1, col_sems).wait_send()

    @pl.when((field == 1) & jnp.logical_not(in_owners))
    def _():
        whole(col_send, owners, col_sems).wait_send()


def dft_constant(nord, lon):
    angles = (np.outer(np.arange(nord), np.arange(lon)) % lon) * (2.0 * math.pi / lon)
    return np.concatenate([np.cos(angles), -np.sin(angles)], axis=0).astype(np.float32).astype(BF)


def fused(lat_count, first, owners, fields_grid, basis, order_table, panel_modes):
    _, snap, _, pairs, lon = fields_grid.shape
    slots, pair_total, degs = basis.shape
    modes = panel_modes.shape[1]
    per = modes // owners
    width = 2 * snap
    block = 2 * slots
    head = pairs * block
    x = fields_grid[0].transpose(0, 2, 1, 3)
    table = jnp.asarray(dft_constant(degs, lon))
    vmem = pl.BlockSpec(memory_space=pltpu.VMEM)
    body = functools.partial(kernel, lat_count, snap, pairs, lon, slots, degs, first, owners, per)
    coef, twice = pl.pallas_call(
        body,
        out_shape=(
            jax.ShapeDtypeStruct((slots, 2 * degs, width), BF),
            jax.ShapeDtypeStruct((2 * modes, width), BF),
        ),
        in_specs=[pl.BlockSpec(memory_space=pl.ANY)] * 5,
        out_specs=(vmem, vmem),
        scratch_shapes=[
            pltpu.VMEM(x.shape, BF),
            pltpu.VMEM(basis.shape, BF),
            pltpu.VMEM(table.shape, BF),
            pltpu.VMEM((slots, lat_count), jnp.int32),
            pltpu.VMEM(panel_modes.shape, jnp.int32),
            pltpu.SemaphoreType.DMA((5,)),
            pltpu.VMEM((lat_count, head, width), BF),
            pltpu.VMEM((lat_count, head, width), BF),
            pltpu.VMEM((owners, pairs * per, width), BF),
            pltpu.VMEM((2, lat_count, pairs * per, width), BF),
            pltpu.VMEM((owners, per, width), BF),
            pltpu.VMEM((lat_count, per, width), BF),
            pltpu.VMEM((2, per, width), BF),
            pltpu.VMEM((owners, per, width), BF),
            pltpu.VMEM((lat_count * head, width), F32),
            pltpu.VMEM((slots, 2 * degs, 2 * pair_total), BF),
        ] + [pltpu.SemaphoreType.DMA] * 3 + [
            pltpu.SemaphoreType.DMA((2,)),
            pltpu.SemaphoreType.DMA,
            pltpu.SemaphoreType.DMA,
            pltpu.SemaphoreType.DMA((2,)),
            pltpu.SemaphoreType.DMA,
            pltpu.SemaphoreType.REGULAR,
        ],
        compiler_params=pltpu.CompilerParams(
            collective_id=0, has_side_effects=True, vmem_limit_bytes=52 * 1024 * 1024
        ),
    )(*[pltpu.with_memory_space_constraint(v, pltpu.HBM) for v in (x, basis, table, order_table.T, panel_modes)])
    panel = lax.dot_general(
        coef.reshape(slots * 2 * degs, width), twice, NT, preferred_element_type=F32
    ) * (1.0 / (snap - 1))
    return panel.astype(BF).reshape(1, slots, 2 * degs, 2 * modes)


def dft_table(orders, lon_count):
    valid_slot = orders >= 0
    safe_orders = jnp.maximum(orders, 0)
    products = lax.broadcasted_iota(jnp.int32, (lon_count, 1), 0) * safe_orders[None, :] % lon_count
    angles = products.astype(jnp.float32) * (2.0 * math.pi / lon_count)
    cosine = jnp.where(valid_slot[None, :], jnp.cos(angles), 0.0).astype(jnp.bfloat16)
    sine_table = jnp.where(valid_slot[None, :], -jnp.sin(angles), 0.0).astype(jnp.bfloat16)
    return jnp.stack([cosine, sine_table], axis=1)


def local(fields_grid, basis, order_table, panel_modes):
    grid_one = fields_grid[0]
    snap_count = grid_one.shape[0]
    pair_count = grid_one.shape[2]
    lon_count = grid_one.shape[3]
    slot_count = order_table.shape[1]
    deg_count = basis.shape[2]
    pair_total = basis.shape[1]
    mode_count = panel_modes.shape[1]
    orders = order_table.reshape(-1)
    slot_all = orders.shape[0]
    dft = dft_table(orders, lon_count)
    fourier = jnp.einsum("thjn,nrk->hkjrt", grid_one, dft, preferred_element_type=jnp.float32) * (
        1.0 / math.sqrt(lon_count)
    )
    fourier = fourier.reshape(2, slot_all, pair_count, 2 * snap_count)
    parity_parts = jnp.stack([fourier[0] + fourier[1], fourier[0] - fourier[1]]).astype(
        jnp.bfloat16
    )
    group_index = lax.axis_index("lat")
    my_orders = lax.dynamic_slice_in_dim(order_table, group_index, 1, 0)[0]
    my_odd = my_orders % 2 == 1
    basis_split = basis.reshape(slot_count, pair_total, deg_count // 2, 2)
    even_rows = basis_split[:, :, :, 0]
    odd_rows = basis_split[:, :, :, 1]
    degree = lax.broadcasted_iota(jnp.int32, (1, deg_count), 1)
    keep_mask = (degree >= my_orders[:, None]) & (my_orders >= 0)[:, None]
    received = lax.all_to_all(parity_parts, "lat", split_axis=1, concat_axis=2, tiled=True)
    first_parity = jnp.where(my_odd[:, None, None], received[1], received[0])
    second = jnp.where(my_odd[:, None, None], received[0], received[1])
    low_degrees = jnp.einsum(
        "sjh,sjc->shc", even_rows, first_parity, preferred_element_type=jnp.float32
    )
    high_degrees = jnp.einsum("sjh,sjc->shc", odd_rows, second, preferred_element_type=jnp.float32)
    joined = jnp.stack([low_degrees, high_degrees], axis=2).reshape(slot_count, deg_count, -1)
    coefficients = jnp.where(keep_mask[:, :, None], joined, 0.0).astype(jnp.bfloat16)
    mode_order = panel_modes[0]
    mode_degree = panel_modes[1]
    onehot = (my_orders[None, :] == mode_order[:, None]).astype(jnp.bfloat16)
    picked = jnp.take(coefficients, mode_degree, axis=1)
    local_values = jnp.einsum("ms,smc->mc", onehot, picked, preferred_element_type=jnp.float32)
    field_index = lax.axis_index("field")
    both_fields = jnp.stack(
        [
            jnp.where(field_index == 0, local_values, 0.0),
            jnp.where(field_index == 1, local_values, 0.0),
        ]
    )
    summed = lax.psum(both_fields, ("lat", "field"))
    other_field = jnp.where(field_index == 0, summed[1], summed[0]).astype(jnp.bfloat16)
    columns = other_field.astype(jnp.float32).reshape(mode_count * 2, snap_count)
    centered = (columns - jnp.mean(columns, axis=1, keepdims=True)).astype(jnp.bfloat16)
    coef_rows = coefficients.reshape(slot_count * deg_count * 2, snap_count)
    panel_values = lax.dot_general(
        coef_rows, centered, (((1,), (1,)), ((), ())), preferred_element_type=jnp.float32
    )
    panel_values = panel_values * (1.0 / (snap_count - 1))
    return panel_values.astype(jnp.bfloat16).reshape(1, slot_count, 2 * deg_count, 2 * mode_count)


def device_program(lat_count, fields_grid, basis, order_table, panel_modes):
    pairs, snap = fields_grid.shape[3], fields_grid.shape[1]
    slots, pair_total, degs = basis.shape
    modes = panel_modes.shape[1]
    first, owners = 1, lat_count // 2
    fits = (
        lat_count % 2 == 0
        and owners > first
        and modes % owners == 0
        and modes // owners == 8
        and 2 * snap == 128
        and slots == 8
        and degs <= 256
        and pair_total <= 2 * snap
        and lat_count * pairs * slots <= 512
    )
    if fits:
        return fused(lat_count, first, owners, fields_grid, basis, order_table, panel_modes)
    return local(fields_grid, basis, order_table, panel_modes)


def solution(mesh):
    placed = (P("field", None, None, "lat", None), P("lat", None, None), P(), P())
    return jax.shard_map(
        functools.partial(device_program, mesh.shape["lat"]),
        mesh=mesh, in_specs=placed, out_specs=P("field", "lat", None, None), check_vma=False,
    )
```

time: 17.9 us -> 16.5 us (0.922)
  Pallas kernels: 16.7 us -> 15.4 us
    pallas_call x1, Pallas kernels: 16.7 us -> 15.4 us  [fused(): pl.pallas_call(body, out_shape=(jax.ShapeDtypeStruct((slots, 2 * degs, wi...]
where the time goes in v1:
time: 16.5 us; the launch traced here: 16.4 us
  Pallas kernels  15.4 us (93%)
  matrix products  1.02 us (6%)
    pallas_call x1, Pallas kernels, fused(): pl.pallas_call(body, out_shape=(jax.ShapeDtypeStruct((slots, 2 * degs, wi...  15.4 us
    dot_general x1, matrix products, fused(): lax.dot_general(coef.reshape(slots * 2 * degs, width), twice, NT, preferr...  1.02 us

profile of v1, /device:TPU:1, one launch (start us, length us, event | category | flops | bytes accessed | tf_op | source)
XLA Modules:
  0.0 16.4 jit_solution(11469537137747794319)
XLA Ops:
  0.0 15.4 %shard_map.55 = (bf16[8,192,128]{2,1,0:T(8,128)(2,1)S(1)}, bf16[128,128]{1,0:T(8,128)(2,1)S(1)}) custom-call(bf16[64,3,2,192]{3,2,1,0:T(2,128)(2,1)} %bitcast.9, bf16[8,48,96]{2,1,0:T(8,128)(2,1)} %basis_hbm.1, bf16[192,192]{1,0:T(8,128)(2,1)} %constant.4.clone.table_hbm, s32[8,16]{1,0:T(8,128)} %bitcast.10, s32[2,64]{1,0:T(2,128)} %modes_hbm.1), custom_call_target="tpu_custom_call" | custom-call | tf_op jit(solution)/shard_map/pallas_call | solution.py:309
  15.4 1.0 %fusion = bf16[1536,128]{1,0:T(8,128)(2,1)} fusion(bf16[1536,128]{1,0:T(8,128)(2,1)S(1)} %bitcast.8, bf16[128,128]{1,0:T(8,128)(2,1)S(1)} %get-tuple-element.8), kind=kOutput, calls=%fused_computation.1 | convolution fusion | flops 50724864 | bytes 819200 | tf_op jit(solution)/shard_map/dot_general | solution.py:346

commit v2 on v1

--- a/solution.py
+++ b/solution.py
@@ -51,7 +51,7 @@
     loads = [
         pltpu.make_async_copy(src, dst, load_sem.at[at])
         for at, (src, dst) in enumerate([
-            (modes_hbm, modes_ref), (orders_hbm, orders_ref), (table_hbm, table_ref),
+            (table_hbm, table_ref), (modes_hbm, modes_ref), (orders_hbm, orders_ref),
             (basis_hbm, basis_ref), (x_hbm, x_ref),
         ])
     ]
@@ -79,8 +79,8 @@
     lax.fori_loop(0, lat_count, greet, 0)
 
     nord = table_ref.shape[0] // 2
-    loads[0].wait()
     loads[1].wait()
+    loads[2].wait()
     diagonal = iota((modes, modes), 0) == iota((modes, modes), 1)
     mode_col = jnp.sum(jnp.where(diagonal, modes_ref[0:1, :], 0), axis=1, keepdims=True)
     deg_col = jnp.sum(jnp.where(diagonal, modes_ref[1:2, :], 0), axis=1, keepdims=True)
@@ -95,7 +95,7 @@
         onehot = (iota((want.shape[0], 2 * nord), 1) == want).astype(F32).astype(BF)
         return mm(onehot, table_ref[...]).astype(BF)
 
-    loads[2].wait()
+    loads[0].wait()
     mode_dft = waves(mode_col, mode_col + nord)
     loads[3].wait()
     cols = jnp.zeros((modes, pair_total), F32)
@@ -127,18 +127,6 @@
         barrier, jnp.where(is_early, early - 1 + across, lat_count - 1 + across_late)
     )
 
-    @pl.when(jnp.logical_not(is_early))
-    def _():
-        def arrive(lat, c):
-            signal(late, lat, field)
-
-            @pl.when((field == 0) & owns(lat))
-            def _():
-                signal(late, lat, other)
-            return c
-
-        lax.fori_loop(0, early, arrive, 0)
-
     def remote(src, dst, sems, lat, core):
         return pltpu.make_async_remote_copy(
             src_ref=src, dst_ref=dst, send_sem=sems[0], recv_sem=sems[1],
@@ -169,6 +157,18 @@
         return c
 
     lax.fori_loop(0, owners, start_tail, 0)
+
+    @pl.when(jnp.logical_not(is_early))
+    def _():
+        def arrive(lat, c):
+            signal(late, lat, field)
+
+            @pl.when((field == 0) & owns(lat))
+            def _():
+                signal(late, lat, other)
+            return c
+
+        lax.fori_loop(0, early, arrive, 0)
 
     tiled = jnp.concatenate([by_slot] * lat_count, axis=0)
     here = iota((slot_all, lat_count), 1) == iota((slot_all, lat_count), 0) // slots
@@ -186,7 +186,7 @@
             remote(send.at[lat], recv.at[me], block_sems, lat, field).start()
         return c
 
-    lax.fori_loop(0, first, start_block, 0)
+    lax.fori_loop(0, 1, start_block, 0)
 
     dup = (iota((2 * degs, degs), 0) // 2 == iota((2 * degs, degs), 1)).astype(F32).astype(BF)
     twin = (iota((pair_total, 2 * pair_total), 1) // 2 == iota((pair_total, 2 * pair_total), 0))
@@ -199,7 +199,9 @@
         keep = (deg >= order) & (order >= 0) & (((deg - order) & 1) == parity)
         rows[s] = jnp.where(keep, base, 0.0).astype(BF)
 
-    lax.fori_loop(first, early, start_block, 0)
+    @pl.when(jnp.logical_not(is_owner))
+    def _():
+        lax.fori_loop(1, early, start_block, 0)
 
     @pl.when(is_early)
     def _():
@@ -240,6 +242,7 @@
         whole(tail_recv.at[0], lat_count, tail_sems(0)).wait_recv()
         mode_send[0] = value_of(0)
         start_mode(1)
+        lax.fori_loop(1, early, start_block, 0)
         mode_recv[me - first] = mode_send[0]
 
     whole(recv, lat_count - 1, block_sems).wait_recv()
@@ -423,7 +426,7 @@
     pairs, snap = fields_grid.shape[3], fields_grid.shape[1]
     slots, pair_total, degs = basis.shape
     modes = panel_modes.shape[1]
-    first, owners = 1, lat_count // 2
+    first, owners = 3, lat_count // 2
     fits = (
         lat_count % 2 == 0
         and owners > first

time: 16.5 us -> 14.2 us (0.86)
  the two profiles are of different devices: /device:TPU:1 before, /device:TPU:0 now
where the time goes in v2:
time: 14.2 us; the launch traced here: 14.1 us
  Pallas kernels  13.1 us (92%)
  matrix products  1.01 us (7%)
    pallas_call x1, Pallas kernels, fused(): pl.pallas_call(body, out_shape=(jax.ShapeDtypeStruct((slots, 2 * degs, wi...  13.1 us
    dot_general x1, matrix products, fused(): lax.dot_general(coef.reshape(slots * 2 * degs, width), twice, NT, preferr...  1.01 us

profile of v2, /device:TPU:0, one launch (start us, length us, event | category | flops | bytes accessed | tf_op | source)
XLA Modules:
  0.0 14.1 jit_solution(95506868335472835)
XLA Ops:
  0.0 13.1 %shard_map.55 = (bf16[8,192,128]{2,1,0:T(8,128)(2,1)S(1)}, bf16[128,128]{1,0:T(8,128)(2,1)S(1)}) custom-call(bf16[64,3,2,192]{3,2,1,0:T(2,128)(2,1)} %bitcast.9, bf16[8,48,96]{2,1,0:T(8,128)(2,1)} %basis_hbm.1, bf16[192,192]{1,0:T(8,128)(2,1)} %constant.4.clone.table_hbm, s32[8,16]{1,0:T(8,128)} %bitcast.10, s32[2,64]{1,0:T(2,128)} %modes_hbm.1), custom_call_target="tpu_custom_call" | custom-call | tf_op jit(solution)/shard_map/pallas_call | solution.py:312
  13.1 1.0 %fusion = bf16[1536,128]{1,0:T(8,128)(2,1)} fusion(bf16[1536,128]{1,0:T(8,128)(2,1)S(1)} %bitcast.8, bf16[128,128]{1,0:T(8,128)(2,1)S(1)} %get-tuple-element.8), kind=kOutput, calls=%fused_computation.1 | convolution fusion | flops 50724864 | bytes 819200 | tf_op jit(solution)/shard_map/dot_general | solution.py:349

commit v3 on v2

--- a/solution.py
+++ b/solution.py
@@ -44,6 +44,8 @@
     slot_all = lat_count * slots
     modes = owners * per
     early = first + owners
+    plane = lat_count // 4
+    inner = me // plane * plane
     is_early = me < early
     in_owners = (me >= first) & (me < early)
     is_owner = in_owners & (field == 1)
@@ -97,14 +99,6 @@
 
     loads[0].wait()
     mode_dft = waves(mode_col, mode_col + nord)
-    loads[3].wait()
-    cols = jnp.zeros((modes, pair_total), F32)
-    at_degree = iota((modes, degs), 1) == deg_col
-    for s in range(slots):
-        pick = at_degree & (mode_col == my_orders[s:s + 1, :])
-        cols = cols + mm_nt(pick.astype(F32).astype(BF), basis_ref[s])
-    cols = jnp.concatenate([cols, jnp.zeros((modes, width - pair_total), F32)], axis=1)
-    col_send[...] = cols.reshape(owners, per, width).astype(BF)
     even_lane = iota((1, width), 1) % 2 == 0
 
     def hemispheres(table, j):
@@ -147,16 +141,31 @@
         return remote(part, part, sems, me, other)
 
     def start_tail(at, c):
-        @pl.when((field == 1) & (at + first != me))
-        def _():
-            remote(col_send.at[at], col_recv.at[me], col_sems, at + first, 1).start()
-
         @pl.when((field == 0) | (at + first != me))
         def _():
             remote(tail_send.at[at], tail_recv.at[field, me], tail_sems(field), at + first, 1).start()
         return c
 
     lax.fori_loop(0, owners, start_tail, 0)
+    loads[3].wait()
+
+    @pl.when(field == 1)
+    def _():
+        cols = jnp.zeros((modes, pair_total), F32)
+        at_degree = iota((modes, degs), 1) == deg_col
+        for s in range(slots):
+            pick = at_degree & (mode_col == my_orders[s:s + 1, :])
+            cols = cols + mm_nt(pick.astype(F32).astype(BF), basis_ref[s])
+        cols = jnp.concatenate([cols, jnp.zeros((modes, width - pair_total), F32)], axis=1)
+        col_send[...] = cols.reshape(owners, per, width).astype(BF)
+
+        def start_col(at, c):
+            @pl.when(at + first != me)
+            def _():
+                remote(col_send.at[at], col_recv.at[me], col_sems, at + first, 1).start()
+            return c
+
+        lax.fori_loop(0, owners, start_col, 0)
 
     @pl.when(jnp.logical_not(is_early))
     def _():
@@ -199,15 +208,22 @@
         keep = (deg >= order) & (order >= 0) & (((deg - order) & 1) == parity)
         rows[s] = jnp.where(keep, base, 0.0).astype(BF)
 
-    @pl.when(jnp.logical_not(is_owner))
-    def _():
-        lax.fori_loop(1, early, start_block, 0)
+    lax.fori_loop(jnp.maximum(inner, 1), early, start_block, 0)
+
+    @pl.when(me < lat_count // 2)
+    def _():
+        lax.fori_loop(1, jnp.minimum(inner, early), start_block, 0)
 
     @pl.when(is_early)
     def _():
         pl.semaphore_wait(late, (lat_count - early) * jnp.where(is_owner, 2, 1))
 
     lax.fori_loop(early, lat_count, start_block, 0)
+
+    @pl.when(jnp.logical_not(is_owner) & (me >= lat_count // 2))
+    def _():
+        lax.fori_loop(1, jnp.minimum(inner, early), start_block, 0)
+
     recv[me] = send[me]
 
     @pl.when(is_owner)
@@ -242,7 +258,11 @@
         whole(tail_recv.at[0], lat_count, tail_sems(0)).wait_recv()
         mode_send[0] = value_of(0)
         start_mode(1)
-        lax.fori_loop(1, early, start_block, 0)
+
+        @pl.when(me >= lat_count // 2)
+        def _():
+            lax.fori_loop(1, jnp.minimum(inner, early), start_block, 0)
+
         mode_recv[me - first] = mode_send[0]
 
     whole(recv, lat_count - 1, block_sems).wait_recv()

time: 14.2 us -> 13.8 us (0.972)
  the two profiles are of different devices: /device:TPU:0 before, /device:TPU:1 now
where the time goes in v3:
time: 13.8 us; the launch traced here: 13.6 us
  Pallas kernels  12.6 us (91%)
  matrix products  1.02 us (7%)
    pallas_call x1, Pallas kernels, fused(): pl.pallas_call(body, out_shape=(jax.ShapeDtypeStruct((slots, 2 * degs, wi...  12.6 us
    dot_general x1, matrix products, fused(): lax.dot_general(coef.reshape(slots * 2 * degs, width), twice, NT, preferr...  1.02 us

profile of v3, /device:TPU:1, one launch (start us, length us, event | category | flops | bytes accessed | tf_op | source)
XLA Modules:
  0.0 13.6 jit_solution(3905323731349375151)
XLA Ops:
  0.0 12.6 %shard_map.55 = (bf16[8,192,128]{2,1,0:T(8,128)(2,1)S(1)}, bf16[128,128]{1,0:T(8,128)(2,1)S(1)}) custom-call(bf16[64,3,2,192]{3,2,1,0:T(2,128)(2,1)} %bitcast.9, bf16[8,48,96]{2,1,0:T(8,128)(2,1)} %basis_hbm.1, bf16[192,192]{1,0:T(8,128)(2,1)} %constant.4.clone.table_hbm, s32[8,16]{1,0:T(8,128)} %bitcast.10, s32[2,64]{1,0:T(2,128)} %modes_hbm.1), custom_call_target="tpu_custom_call" | custom-call | tf_op jit(solution)/shard_map/pallas_call | solution.py:332
  12.6 1.0 %fusion = bf16[1536,128]{1,0:T(8,128)(2,1)} fusion(bf16[1536,128]{1,0:T(8,128)(2,1)S(1)} %bitcast.8, bf16[128,128]{1,0:T(8,128)(2,1)S(1)} %get-tuple-element.8), kind=kOutput, calls=%fused_computation.1 | convolution fusion | flops 50724864 | bytes 819200 | tf_op jit(solution)/shard_map/dot_general | solution.py:369

commit v4 on v3

--- a/solution.py
+++ b/solution.py
@@ -33,7 +33,7 @@
     x_ref, basis_ref, table_ref, orders_ref, modes_ref, load_sem,
     send, recv, tail_send, tail_recv, col_send, col_recv, mode_send, mode_recv, wide, rows,
     send_sem, recv_sem, tail_send_sem, tail_recv_sem, col_send_sem, col_recv_sem,
-    mode_send_sem, mode_recv_sem, late,
+    mode_send_sem, mode_recv_sem, late, ready,
 ):
     me = lax.axis_index("lat")
     field = lax.axis_index("field")
@@ -69,7 +69,7 @@
         return (lat >= first) & (lat < early)
 
     def greet(lat, c):
-        @pl.when((lat != me) & (is_early | (lat >= early)))
+        @pl.when((lat != me) & is_early)
         def _():
             signal(barrier, lat, field)
 
@@ -118,7 +118,7 @@
     across = jnp.where(field == 0, owners, jnp.where(is_owner, early, 0))
     across_late = jnp.where(field == 0, owners, 0)
     pl.semaphore_wait(
-        barrier, jnp.where(is_early, early - 1 + across, lat_count - 1 + across_late)
+        barrier, jnp.where(is_early, early - 1 + across, early + across_late)
     )
 
     def remote(src, dst, sems, lat, core):
@@ -218,11 +218,24 @@
     def _():
         pl.semaphore_wait(late, (lat_count - early) * jnp.where(is_owner, 2, 1))
 
-    lax.fori_loop(early, lat_count, start_block, 0)
+        @pl.when(me == early - 1)
+        def _():
+            def tell(lat, c):
+                signal(ready, lat, field)
+                return c
+
+            lax.fori_loop(early, lat_count, tell, 0)
+
+        lax.fori_loop(early, lat_count, start_block, 0)
 
     @pl.when(jnp.logical_not(is_owner) & (me >= lat_count // 2))
     def _():
         lax.fori_loop(1, jnp.minimum(inner, early), start_block, 0)
+
+    @pl.when(jnp.logical_not(is_early))
+    def _():
+        pl.semaphore_wait(ready, 1)
+        lax.fori_loop(early, lat_count, start_block, 0)
 
     recv[me] = send[me]
 
@@ -265,31 +278,45 @@
 
         mode_recv[me - first] = mode_send[0]
 
-    whole(recv, lat_count - 1, block_sems).wait_recv()
-    wide[...] = recv[...].reshape(slot_all * 2 * pairs, width).astype(F32)
-    same_r = iota((2 * degs, width), 1) % 2 == iota((2 * degs, width), 0) % 2
-    for s in range(slots):
-        picked = wide[pl.ds(s, 2 * pair_total, stride=slots), :].astype(BF)
-        coef_ref[s] = jnp.where(same_r, mm(rows[s], picked), 0.0).astype(BF)
-
     expand = (iota((2 * modes, modes), 1) == iota((2 * modes, modes), 0) // 2).astype(F32).astype(BF)
     u_match = iota((2 * modes, width), 1) % 2 == iota((2 * modes, width), 0) % 2
     row_even = iota((2 * modes, 1), 0) % 2 == 0
-
-    @pl.when(is_owner)
-    def _():
-        whole(mode_recv, owners - 1, mode_sems(0)).wait_recv()
-
-    @pl.when(jnp.logical_not(is_owner))
-    def _():
-        whole(mode_recv, owners, mode_sems(0)).wait_recv()
-
-    columns = mm(expand, mode_recv[...].reshape(modes, width))
-    masked = jnp.where(u_match, columns, 0.0)
-    mean = jnp.sum(masked, axis=1, keepdims=True) * (1.0 / snap)
-    centered = jnp.where(u_match, masked - mean, 0.0)
-    moved = jnp.where(row_even, pltpu.roll(centered, 1, 1), pltpu.roll(centered, width - 1, 1))
-    twice_ref[...] = (centered + moved).astype(BF)
+    same_r = iota((2 * degs, width), 1) % 2 == iota((2 * degs, width), 0) % 2
+
+    def take_blocks():
+        whole(recv, lat_count - 1, block_sems).wait_recv()
+        wide[...] = recv[...].reshape(slot_all * 2 * pairs, width).astype(F32)
+        for s in range(slots):
+            picked = wide[pl.ds(s, 2 * pair_total, stride=slots), :].astype(BF)
+            coef_ref[s] = jnp.where(same_r, mm(rows[s], picked), 0.0).astype(BF)
+
+    def take_modes():
+        @pl.when(is_owner)
+        def _():
+            whole(mode_recv, owners - 1, mode_sems(0)).wait_recv()
+
+        @pl.when(jnp.logical_not(is_owner))
+        def _():
+            whole(mode_recv, owners, mode_sems(0)).wait_recv()
+
+        columns = mm(expand, mode_recv[...].reshape(modes, width))
+        masked = jnp.where(u_match, columns, 0.0)
+        mean = jnp.sum(masked, axis=1, keepdims=True) * (1.0 / snap)
+        centered = jnp.where(u_match, masked - mean, 0.0)
+        moved = jnp.where(row_even, pltpu.roll(centered, 1, 1), pltpu.roll(centered, width - 1, 1))
+        twice_ref[...] = (centered + moved).astype(BF)
+
+    modes_first = (me > 0) & (me < lat_count // 2)
+
+    @pl.when(modes_first)
+    def _():
+        take_modes()
+        take_blocks()
+
+    @pl.when(jnp.logical_not(modes_first))
+    def _():
+        take_blocks()
+        take_modes()
 
     whole(send, lat_count - 1, block_sems).wait_send()
 
@@ -361,6 +388,7 @@
             pltpu.SemaphoreType.DMA((2,)),
             pltpu.SemaphoreType.DMA,
             pltpu.SemaphoreType.REGULAR,
+            pltpu.SemaphoreType.REGULAR,
         ],
         compiler_params=pltpu.CompilerParams(
             collective_id=0, has_side_effects=True, vmem_limit_bytes=52 * 1024 * 1024

time: 13.8 us -> 13.8 us (level)
  no operation moved by 1% of the time
where the time goes in v4:
time: 13.8 us; the launch traced here: 13.6 us
  Pallas kernels  12.6 us (91%)
  matrix products  1.01 us (7%)
    pallas_call x1, Pallas kernels, fused(): pl.pallas_call(body, out_shape=(jax.ShapeDtypeStruct((slots, 2 * degs, wi...  12.6 us
    dot_general x1, matrix products, fused(): lax.dot_general(coef.reshape(slots * 2 * degs, width), twice, NT, preferr...  1.01 us

profile of v4, /device:TPU:1, one launch (start us, length us, event | category | flops | bytes accessed | tf_op | source)
XLA Modules:
  0.0 13.6 jit_solution(3878828826629689931)
XLA Ops:
  0.0 12.6 %shard_map.55 = (bf16[8,192,128]{2,1,0:T(8,128)(2,1)S(1)}, bf16[128,128]{1,0:T(8,128)(2,1)S(1)}) custom-call(bf16[64,3,2,192]{3,2,1,0:T(2,128)(2,1)} %bitcast.9, bf16[8,48,96]{2,1,0:T(8,128)(2,1)} %basis_hbm.1, bf16[192,192]{1,0:T(8,128)(2,1)} %constant.4.clone.table_hbm, s32[8,16]{1,0:T(8,128)} %bitcast.10, s32[2,64]{1,0:T(2,128)} %modes_hbm.1), custom_call_target="tpu_custom_call" | custom-call | tf_op jit(solution)/shard_map/pallas_call | solution.py:359
  12.6 1.0 %fusion = bf16[1536,128]{1,0:T(8,128)(2,1)} fusion(bf16[1536,128]{1,0:T(8,128)(2,1)S(1)} %bitcast.8, bf16[128,128]{1,0:T(8,128)(2,1)S(1)} %get-tuple-element.8), kind=kOutput, calls=%fused_computation.1 | convolution fusion | flops 50724864 | bytes 819200 | tf_op jit(solution)/shard_map/dot_general | solution.py:397

commit v5 on v4

--- a/solution.py
+++ b/solution.py
@@ -46,6 +46,7 @@
     early = first + owners
     plane = lat_count // 4
     inner = me // plane * plane
+    outer = lat_count - plane
     is_early = me < early
     in_owners = (me >= first) & (me < early)
     is_owner = in_owners & (field == 1)
@@ -68,7 +69,9 @@
     def owns(lat):
         return (lat >= first) & (lat < early)
 
-    def greet(lat, c):
+    def greet(at, c):
+        lat = lat_count - 1 - at
+
         @pl.when((lat != me) & is_early)
         def _():
             signal(barrier, lat, field)
@@ -78,7 +81,7 @@
             signal(barrier, lat, other)
         return c
 
-    lax.fori_loop(0, lat_count, greet, 0)
+    lax.fori_loop(0, lat_count, greet, 0, unroll=True)
 
     nord = table_ref.shape[0] // 2
     loads[1].wait()
@@ -226,7 +229,11 @@
 
             lax.fori_loop(early, lat_count, tell, 0)
 
-        lax.fori_loop(early, lat_count, start_block, 0)
+        lax.fori_loop(outer, jnp.where(is_owner, outer + 1, outer), start_block, 0)
+
+        @pl.when(jnp.logical_not(is_owner))
+        def _():
+            lax.fori_loop(early, lat_count, start_block, 0)
 
     @pl.when(jnp.logical_not(is_owner) & (me >= lat_count // 2))
     def _():
@@ -276,6 +283,8 @@
         def _():
             lax.fori_loop(1, jnp.minimum(inner, early), start_block, 0)
 
+        lax.fori_loop(early, outer, start_block, 0)
+        lax.fori_loop(outer + 1, lat_count, start_block, 0)
         mode_recv[me - first] = mode_send[0]
 
     expand = (iota((2 * modes, modes), 1) == iota((2 * modes, modes), 0) // 2).astype(F32).astype(BF)

time: 13.8 us -> 13.8 us (level)
  no operation moved by 1% of the time
where the time goes in v5:
time: 13.8 us; the launch traced here: 13.7 us
  Pallas kernels  12.7 us (92%)
  matrix products  1.02 us (7%)
    pallas_call x1, Pallas kernels, fused(): pl.pallas_call(body, out_shape=(jax.ShapeDtypeStruct((slots, 2 * degs, wi...  12.7 us
    dot_general x1, matrix products, fused(): lax.dot_general(coef.reshape(slots * 2 * degs, width), twice, NT, preferr...  1.02 us

profile of v5, /device:TPU:1, one launch (start us, length us, event | category | flops | bytes accessed | tf_op | source)
XLA Modules:
  0.0 13.7 jit_solution(5094810070795379012)
XLA Ops:
  0.0 12.7 %shard_map.55 = (bf16[8,192,128]{2,1,0:T(8,128)(2,1)S(1)}, bf16[128,128]{1,0:T(8,128)(2,1)S(1)}) custom-call(bf16[64,3,2,192]{3,2,1,0:T(2,128)(2,1)} %bitcast.9, bf16[8,48,96]{2,1,0:T(8,128)(2,1)} %basis_hbm.1, bf16[192,192]{1,0:T(8,128)(2,1)} %constant.4.clone.table_hbm, s32[8,16]{1,0:T(8,128)} %bitcast.10, s32[2,64]{1,0:T(2,128)} %modes_hbm.1), custom_call_target="tpu_custom_call" | custom-call | tf_op jit(solution)/shard_map/pallas_call | solution.py:368
  12.7 1.0 %fusion = bf16[1536,128]{1,0:T(8,128)(2,1)} fusion(bf16[1536,128]{1,0:T(8,128)(2,1)S(1)} %bitcast.8, bf16[128,128]{1,0:T(8,128)(2,1)S(1)} %get-tuple-element.8), kind=kOutput, calls=%fused_computation.1 | convolution fusion | flops 50724864 | bytes 819200 | tf_op jit(solution)/shard_map/dot_general | solution.py:406
